TPU v7x, 512 devices: a whole 4x8x8 slice. The times are simulated.
512 devices in a mesh: dp: 4 (over x), expert: 32 (over z, y_lo), tensor: 4 (over y_hi, core).
Axes of the slice: x: 4, y: 8 (y_hi: 2, y_lo: 4; y = y_hi * 4 + y_lo), z: 8, core: 2. Of those that a mesh axis runs over, the one named last changes fastest.
Arguments:
- tokens: bfloat16 [16384, 7168], P(('dp', 'expert'), 'tensor'), may hold values from -6 to 6
- expert_ids: int32 [16384, 2], P(('dp', 'expert')), may hold values from 0 to 31, all different within a row; in each aligned block of 128 rows (0 to 127, 128 to 255, ...) at most 12 rows name the same one
- gate_scores: bfloat16 [16384, 2], P(('dp', 'expert')), may hold values from 0.099609375 to 0.59765625
- weight_in: bfloat16 [32, 2, 7168, 1024], P('expert', None, 'tensor', 'dp'), may hold values from -0.0625 to 0.0625
- weight_out: bfloat16 [32, 1024, 7168], P('expert', 'dp', 'tensor'), may hold values from -0.1875 to 0.1875
Outputs:
- mixed: bfloat16 [16384, 7168], P(('dp', 'expert'), 'tensor')
Inputs may be any that keep to these rules, and one draw needn't show every extreme that they name: `expert_ids`: each token names 2 different experts; among the 128 tokens of one index of dp and expert together (aligned blocks of rows) no expert is named more than 12 times, and in some blocks an expert is named exactly 12 times.
All inputs are finite; a program needn't handle non-finite values.
Results may differ from a plain program's by a relative error of at most 0.0071.
Values may be sent and summed in bfloat16 or wider, within the bound.
No kernel may reach another device: no remote copies, remote signals or barrier semaphores. Data moves between devices by JAX's collectives and lax.ppermute only.
A program may use at most 64 MiB of HBM per device.

v0:
```python
import jax
import jax.numpy as jnp
from jax import lax
from jax.sharding import Mesh
from jax.sharding import PartitionSpec as P

TENSOR = ("tensor_0", "tensor_1")


def one_axis_at_a_time(shard, axes):
    for axis in axes:
        shard = lax.psum(shard, axis)
    return shard


def in_blocks(shard, dim, devices):
    before, after = (shard.shape[:dim], shard.shape[dim + 1 :])
    return jnp.moveaxis(shard.reshape(*before, devices, -1, *after), dim, 0)


def sent_and_summed(shard, axis, dim):
    devices = lax.axis_size(axis)
    pieces = lax.all_to_all(in_blocks(shard, dim, devices), axis, 0, 0, tiled=True)
    return jnp.sum(pieces, axis=0)


def joined_along(pieces, dim):
    dims = list(pieces.shape[1:])
    dims[dim] *= pieces.shape[0]
    return jnp.moveaxis(pieces, 0, dim).reshape(dims)


def gather_in_order(shard, axes, order):
    pieces = shard[None]
    for k in order:
        pieces = lax.all_gather(pieces, axes[k], axis=0, tiled=True)
    held = [lax.axis_size(axes[k]) for k in reversed(order)]
    pieces = pieces.reshape(*held, *shard.shape)
    turned = sorted(range(len(order)), key=lambda place: order[len(order) - 1 - place])
    return pieces.transpose(*turned, *range(len(order), pieces.ndim)).reshape(-1, *shard.shape)


def gathered_by_axis(shard, axes, order, dim):
    return joined_along(gather_in_order(shard, axes, order), dim)


def per_device(tokens, expert_ids, gate_scores, weight_in, weight_out):
    experts = lax.axis_size("expert")
    tok_count, top_count = expert_ids.shape
    capacity = min(3 * tok_count * top_count // (2 * experts), tok_count)
    width_all = tokens.shape[1] * lax.axis_size(TENSOR)
    wide = tokens.astype(jnp.float32)
    row_squares = one_axis_at_a_time(jnp.sum(wide * wide, axis=1, keepdims=True), TENSOR)
    normed = (wide * lax.rsqrt(row_squares / width_all + 1e-06)).astype(jnp.bfloat16)
    flat_ids = expert_ids.reshape(-1)
    one_hot = (flat_ids[:, None] == jnp.arange(experts, dtype=jnp.int32)[None, :]).astype(jnp.int32)
    earlier = jnp.cumsum(one_hot, axis=0) - one_hot
    slot_pos = jnp.sum(earlier * one_hot, axis=1)
    target = flat_ids * capacity + slot_pos
    chosen = (target[:, None] == jnp.arange(experts * capacity, dtype=jnp.int32)[None, :]).astype(
        jnp.float32
    )
    chosen = chosen.reshape(tok_count, top_count, experts * capacity)
    picked = jnp.sum(chosen, axis=1).astype(jnp.bfloat16)
    combine_weight = jnp.sum(chosen * gate_scores.astype(jnp.float32)[:, :, None], axis=1).astype(
        jnp.bfloat16
    )
    outgoing = jnp.einsum("ts,td->sd", picked, normed, preferred_element_type=jnp.float32).astype(
        jnp.bfloat16
    )
    outgoing = outgoing.reshape(experts, capacity, tokens.shape[1])
    arrived = lax.all_to_all(outgoing, "expert", split_axis=0, concat_axis=0, tiled=True)
    slot_rows = arrived.reshape(experts * capacity, tokens.shape[1])
    local_in = weight_in[0]
    partial_sums = jnp.einsum(
        "rd,gdf->rgf",
        slot_rows,
        lax.all_gather(local_in, "dp", axis=2, tiled=True),
        preferred_element_type=jnp.float32,
    )
    summed = sent_and_summed(partial_sums, TENSOR, 2)
    hidden = (jax.nn.silu(summed[:, 0]) * summed[:, 1]).astype(jnp.bfloat16)
    hidden = hidden[:, None, :]
    row_count = hidden.shape[0]
    hidden_full = gathered_by_axis(hidden, TENSOR, (0, 1), 2).reshape(row_count, -1)
    expert_out = jnp.dot(
        hidden_full,
        lax.all_gather(weight_out[0], "dp", axis=0, tiled=True),
        preferred_element_type=jnp.float32,
    )
    sending = expert_out.astype(jnp.bfloat16).reshape(experts, capacity, weight_out.shape[2])
    returned = lax.all_to_all(sending, "expert", split_axis=0, concat_axis=0, tiled=True)
    mixed = jnp.dot(
        combine_weight,
        returned.reshape(experts * capacity, weight_out.shape[2]),
        preferred_element_type=jnp.float32,
    )
    return mixed.astype(jnp.bfloat16)


def solution(mesh):
    finer = Mesh(
        mesh.devices.reshape(mesh.shape["dp"], mesh.shape["expert"], 2, 2),
        ("dp", "expert", "tensor_0", "tensor_1"),
    )
    placed = (
        P(("dp", "expert"), TENSOR),
        P(("dp", "expert"), None),
        P(("dp", "expert"), None),
        P("expert", None, TENSOR, "dp"),
        P("expert", "dp", TENSOR),
    )
    return jax.shard_map(
        per_device,
        mesh=finer,
        in_specs=placed,
        out_specs=P(("dp", "expert"), TENSOR),
        check_vma=False,
    )
```

profile of v0, /device:TPU:16, one launch (start us, length us, event | category | flops | bytes accessed | tf_op | source)
XLA Modules:
  0.0 282.2 jit_solution(8761266857783817856)
XLA Ops:
  6.5 0.0 copy-start.1
  6.5 0.0 copy-start.2
  6.5 0.0 copy-start
  6.5 0.0 all-gather.5.cloned.1.call-start
  6.5 0.7 all-gather.5.cloned.1.call-update
  7.3 0.0 copy-done.1
  7.3 0.1 copy.47
  7.4 0.1 eq.39
  7.5 0.1 eq.43
  7.7 0.0 copy-done.2
  7.7 0.6 reduce-window.6
  8.3 0.2 slice_reduce_fusion
  8.5 0.1 fusion.16
  8.6 0.1 reduce_sum.48
  8.8 0.1 copy.50
  8.8 0.0 copy-done
  8.8 0.2 fusion.6
  9.0 8.8 %psum.14 = f32[128,1]{0,1:T(1,128)S(1)} all-reduce(f32[128,1]{0,1:T(1,128)S(1)} %bitcast.63), channel_id=1, replica_groups=mesh['dp'=4,'expert'=32,'tensor_0'=2,'tensor_1'=2] {'tensor_0'}, use_global_device_ids=true, to_apply=%region_6.7 | all-reduce | flops 128 | bytes 1024 | tf_op jit(solution)/shard_map/psum | solution.py:12
  17.9 2.4 psum.15
  20.3 0.1 select_reduce_fusion
  20.5 0.6 convolution_convert_fusion
  21.1 1.5 reshape.98
  22.6 13.8 %all-to-all-start = ((bf16[32,12,1792]{2,1,0:T(8,128)(2,1)}), bf16[32,12,1792]{2,1,0:T(8,128)(2,1)S(1)}, u32[]{:S(2)}, u32[]{:S(2)}) async-start(bf16[32,12,1792]{2,1,0:T(8,128)(2,1)} %reshape.98), calls=%async_computation | async-start | bytes 3670016 | tf_op jit(solution)/shard_map/all_to_all | solution.py:72
  36.4 0.0 all-gather.7.cloned.1.call-start
  36.5 0.7 all-gather.7.cloned.1.call-update
  37.2 43.4 %all-to-all-done = bf16[32,12,1792]{2,1,0:T(8,128)(2,1)S(1)} async-done(((bf16[32,12,1792]{2,1,0:T(8,128)(2,1)}), bf16[32,12,1792]{2,1,0:T(8,128)(2,1)S(1)}, u32[]{:S(2)}, u32[]{:S(2)}) %all-to-all-start) | async-done | bytes 1376288 | tf_op jit(solution)/shard_map/all_to_all | solution.py:72
  80.6 0.3 reshape.106
  80.9 16.9 %all-gather.5.cloned.1.call-done = bf16[1,2,1792,1024]{3,2,1,0:T(8,128)(2,1)} async-done(((bf16[1,2,1792,256]{3,2,1,0:T(8,128)(2,1)}), bf16[1,2,1792,1024]{3,2,1,0:T(8,128)(2,1)}) %all-gather.5.cloned.1.call-update) | async-done | bytes 7340048 | tf_op jit(solution)/shard_map/all_gather | solution.py:78
  97.9 10.1 %copy.51 = bf16[2,1024,1792]{2,1,0:T(8,128)(2,1)} copy(bf16[2,1024,1792]{1,2,0:T(8,128)(2,1)} %bitcast.58) | data formatting | bytes 14680064 | tf_op jit(solution)/shard_map/rd,gdf->rgf/dot_general | solution.py:75
  107.9 5.3 %convolution_bitcast_fusion = f32[4,384,2,256]{3,1,0,2:T(8,128)S(1)} fusion(bf16[2,4,256,1792]{3,2,1,0:T(8,128)(2,1)} %bitcast.59, bf16[384,1792,1,1]{1,0,2,3:T(8,128)(2,1)S(1)} %reshape.106), kind=kOutput, calls=%fused_computation.5 | convolution fusion | flops 2818572288 | bytes 11862016 | tf_op jit(solution)/shard_map/rd,gdf->rgf/dot_general | solution.py:75
  113.2 0.2 copy.52
  113.5 79.2 %all_to_all.15 = f32[4,384,2,256]{3,1,2,0:T(8,128)S(1)} all-to-all(f32[4,384,2,256]{3,1,2,0:T(8,128)S(1)} %copy.52), channel_id=1, replica_groups=mesh['dp'=4,'expert'=32,'tensor_0'=2,'tensor_1'=2] {'tensor_0','tensor_1'}, dimensions={0} | all-to-all | bytes 6291456 | tf_op jit(solution)/shard_map/all_to_all | solution.py:23
  192.7 1.2 reduce_sum.52
  193.8 1.2 fusion.11
  195.0 14.9 %all_gather.13 = bf16[2,384,1,256]{3,1,2,0:T(8,128)(2,1)S(1)} all-gather(bf16[1,384,1,256]{3,1,2,0:T(8,128)(2,1)S(1)} %fusion.11), channel_id=1, replica_groups=mesh['dp'=4,'expert'=32,'tensor_0'=2,'tensor_1'=2] {'tensor_0'}, dimensions={0}, use_global_device_ids=true | all-gather | bytes 589824 | tf_op jit(solution)/shard_map/all_gather | solution.py:36
  209.9 2.4 all_gather.14
  212.3 0.1 copy.53
  212.3 0.4 copy.54
  212.7 0.0 all-gather.7.cloned.1.call-done
  212.7 3.7 %fusion.2 = bf16[384,1792]{1,0:T(8,128)(2,1)S(1)} fusion(bf16[384,1024]{0,1:T(8,128)(2,1)S(1)} %bitcast.62, bf16[1,1024,1792]{2,1,0:T(8,128)(2,1)} %all-gather.7.cloned.1.call-done), kind=kOutput, calls=%fused_computation.3 | convolution fusion | flops 1409974272 | bytes 5832704 | tf_op jit(solution)/shard_map/dot_general | solution.py:86
  216.4 0.4 reshape.102
  216.8 55.0 %all_to_all.16 = bf16[32,12,1792]{2,1,0:T(8,128)(2,1)} all-to-all(bf16[32,12,1792]{2,1,0:T(8,128)(2,1)S(1)} %reshape.102), channel_id=1, replica_groups=mesh['dp'=4,'expert'=32,'tensor_0'=2,'tensor_1'=2] {'expert'}, dimensions={0} | all-to-all | bytes 2752512 | tf_op jit(solution)/shard_map/all_to_all | solution.py:92
  271.8 2.4 reshape.103
  274.1 1.2 convolution_convert_fusion.1
  (6 shorter events, 0.1 us)
Async XLA Ops:
  6.5 0.7 copy-start.1
  6.5 1.1 copy-start.2
  6.5 2.3 copy-start
  6.5 91.3 %all-gather.5.cloned.1.call-start = ((), (), s32[]{:S(2)}) async-start(), calls=%async_computation.3 | async-start | bytes 9175040 | tf_op jit(solution)/shard_map/all_gather | solution.py:78
  22.6 58.0 %all-to-all-start = ((bf16[32,12,1792]{2,1,0:T(8,128)(2,1)}), bf16[32,12,1792]{2,1,0:T(8,128)(2,1)S(1)}, u32[]{:S(2)}, u32[]{:S(2)}) async-start(bf16[32,12,1792]{2,1,0:T(8,128)(2,1)} %reshape.98), calls=%async_computation | async-start | bytes 3670016 | tf_op jit(solution)/shard_map/all_to_all | solution.py:72
  36.4 176.3 %all-gather.7.cloned.1.call-start = ((), (), s32[]{:S(2)}) async-start(), calls=%async_computation.4 | async-start | bytes 4587520 | tf_op jit(solution)/shard_map/all_gather | solution.py:88
Sparse Core Ops, SparseCore 0:
  9.5 88.3 all-gather.4
  100.0 49.7 all-gather.6
where the time goes:
time: 283 us; the launch traced here: 282 us
  blocking collectives  163 us (58%)
  waiting for transfers between devices  61.7 us (22%)
  local copies, waits for them, and re-layouts  16 us (6%)
  starting transfers between devices  13.9 us (5%)
  between operations  13.6 us (5%)
  matrix products  10.7 us (4%)
  other arithmetic  3.46 us (1%)
    all_to_all x1, blocking collectives, sent_and_summed(): lax.all_to_all(in_blocks(shard, dim, devices), axis, 0, 0, tiled=True)  79.2 us
    all_to_all x1, blocking collectives, per_device(): lax.all_to_all(sending, 'expert', split_axis=0, concat_axis=0, tiled=True)  55 us
    all_to_all x1, waiting for transfers between devices, per_device(): lax.all_to_all(outgoing, 'expert', split_axis=0, concat_axis=0, tiled=True)  43.4 us
    all_gather x2, blocking collectives, gather_in_order(): pieces = lax.all_gather(pieces, axes[k], axis=0, tiled=True)  17.2 us
    all_gather x1, waiting for transfers between devices, per_device(): lax.all_gather(local_in, 'dp', axis=2, tiled=True)  16.9 us
    all_to_all x1, starting transfers between devices, per_device(): lax.all_to_all(outgoing, 'expert', split_axis=0, concat_axis=0, tiled=True)  13.8 us
    psum x2, blocking collectives, one_axis_at_a_time(): shard = lax.psum(shard, axis)  11.3 us
    dot_general x1, local copies, waits for them, and re-layouts, per_device(): jnp.einsum('rd,gdf->rgf', slot_rows, lax.all_gather(local_in, 'dp', axis=...  10.1 us
  transfers between devices with their start and end apart: 3, of which 2 were waited for; matrix products, arithmetic and copies ran while one was open for 8% of the time, Pallas kernels for 0%

commit v1 on v0

--- a/solution.py
+++ b/solution.py
@@ -75,7 +75,9 @@
     partial_sums = jnp.einsum(
         "rd,gdf->rgf",
         slot_rows,
-        lax.all_gather(local_in, "dp", axis=2, tiled=True),
+        jnp.concatenate(
+            lax.all_to_all(jnp.stack([local_in] * lax.axis_size("dp")), "dp", 0, 0), axis=2
+        ),
         preferred_element_type=jnp.float32,
     )
     summed = sent_and_summed(partial_sums, TENSOR, 2)

time: 283 us -> 377 us (1.33)
  waiting for transfers between devices: 61.7 us -> 151 us
  starting transfers between devices: 13.9 us -> 19.4 us
    all_to_all x0 -> x1, waiting for transfers between devices: none -> 110 us  [per_device(): lax.all_to_all(jnp.stack([local_in] * lax.axis_size('dp')), 'dp', 0, 0)]
    all_to_all x1, blocking collectives: 79.2 us -> 57.9 us  [sent_and_summed(): lax.all_to_all(in_blocks(shard, dim, devices), axis, 0, 0, tiled=True)]
    all_gather x1 -> x0, waiting for transfers between devices: 16.9 us -> none  [per_device(): lax.all_gather(local_in, 'dp', axis=2, tiled=True)]
    dot_general x1 -> x0, local copies, waits for them, and re-layouts: 10.1 us -> none  [per_device(): jnp.einsum('rd,gdf->rgf', slot_rows, lax.all_gather(local_in, 'dp', axis=...]
    all_to_all x1, blocking collectives: 55 us -> 64.4 us  [per_device(): lax.all_to_all(sending, 'expert', split_axis=0, concat_axis=0, tiled=True)]
    another operation x1 -> x3, local copies, waits for them, and re-layouts: 0.01 us -> 8.85 us  [the longest x1 4.95 us: per_device(): jnp.stack([local_in] * lax.axis_size('dp'))]
    all_gather x2, blocking collectives: 17.2 us -> 25.9 us  [gather_in_order(): pieces = lax.all_gather(pieces, axes[k], axis=0, tiled=True)]
    all_to_all x0 -> x1, starting transfers between devices: none -> 5.52 us  [per_device(): lax.all_to_all(jnp.stack([local_in] * lax.axis_size('dp')), 'dp', 0, 0)]
  transfers between devices with their start and end apart: 3 -> 3, of which waited for: 2 -> 2; matrix products, arithmetic and copies ran while one was open for 8% -> 3% of each run, Pallas kernels for 0% -> 0%
where the time goes in v1:
time: 377 us; the launch traced here: 376 us
  blocking collectives  160 us (42%)
  waiting for transfers between devices  151 us (40%)
  starting transfers between devices  19.4 us (5%)
  local copies, waits for them, and re-layouts  15.4 us (4%)
  between operations  13.5 us (4%)
  matrix products  11.7 us (3%)
  other arithmetic  5.82 us (2%)
    all_to_all x1, waiting for transfers between devices, per_device(): lax.all_to_all(jnp.stack([local_in] * lax.axis_size('dp')), 'dp', 0, 0)  110 us
    all_to_all x1, blocking collectives, per_device(): lax.all_to_all(sending, 'expert', split_axis=0, concat_axis=0, tiled=True)  64.4 us
    all_to_all x1, blocking collectives, sent_and_summed(): lax.all_to_all(in_blocks(shard, dim, devices), axis, 0, 0, tiled=True)  57.9 us
    all_to_all x1, waiting for transfers between devices, per_device(): lax.all_to_all(outgoing, 'expert', split_axis=0, concat_axis=0, tiled=True)  40.3 us
    all_gather x2, blocking collectives, gather_in_order(): pieces = lax.all_gather(pieces, axes[k], axis=0, tiled=True)  25.9 us
    all_to_all x1, starting transfers between devices, per_device(): lax.all_to_all(outgoing, 'expert', split_axis=0, concat_axis=0, tiled=True)  13.8 us
    psum x2, blocking collectives, one_axis_at_a_time(): shard = lax.psum(shard, axis)  11.3 us
  transfers between devices with their start and end apart: 3, of which 2 were waited for; matrix products, arithmetic and copies ran while one was open for 3% of the time, Pallas kernels for 0%

profile of v1, /device:TPU:16, one launch (start us, length us, event | category | flops | bytes accessed | tf_op | source)
XLA Modules:
  0.0 376.3 jit_solution(8469246885728399271)
XLA Ops:
  6.5 0.8 copy.59
  7.3 0.1 eq.39
  7.5 0.1 eq.43
  7.6 1.2 fusion.12
  8.8 8.8 %psum.14 = f32[128,1]{0,1:T(1,128)S(1)} all-reduce(f32[128,1]{0,1:T(1,128)S(1)} %bitcast.69), channel_id=1, replica_groups=mesh['dp'=4,'expert'=32,'tensor_0'=2,'tensor_1'=2] {'tensor_0'}, use_global_device_ids=true, to_apply=%region_6.7 | all-reduce | flops 128 | bytes 1024 | tf_op jit(solution)/shard_map/psum | solution.py:12
  17.6 2.4 psum.15
  20.1 0.7 convert_element_type.47
  20.8 0.6 reduce-window.6
  21.4 0.2 slice_reduce_fusion
  21.6 0.1 fusion.22
  21.7 0.1 reduce_sum.48
  21.8 0.1 copy.62
  21.9 0.7 multiply_add_fusion
  22.6 0.1 select_reduce_fusion
  22.7 1.6 convolution_convert_fusion
  24.4 1.4 reshape.105
  25.8 13.8 %all-to-all-start = ((bf16[32,12,1792]{2,1,0:T(8,128)(2,1)}), bf16[32,12,1792]{2,1,0:T(8,128)(2,1)S(1)}, u32[]{:S(2)}, u32[]{:S(2)}) async-start(bf16[32,12,1792]{2,1,0:T(8,128)(2,1)} %reshape.105), calls=%async_computation | async-start | bytes 3670016 | tf_op jit(solution)/shard_map/all_to_all | solution.py:72
  39.6 3.9 %copy.63 = bf16[2,1792,256]{1,2,0:T(8,128)(2,1)} copy(bf16[2,1792,256]{2,1,0:T(8,128)(2,1)} %bitcast.67) | data formatting | bytes 3670016 | tf_op jit(solution)/shard_map/shard_map
  43.5 40.3 %all-to-all-done = bf16[32,12,1792]{2,1,0:T(8,128)(2,1)S(1)} async-done(((bf16[32,12,1792]{2,1,0:T(8,128)(2,1)}), bf16[32,12,1792]{2,1,0:T(8,128)(2,1)S(1)}, u32[]{:S(2)}, u32[]{:S(2)}) %all-to-all-start) | async-done | bytes 1376288 | tf_op jit(solution)/shard_map/all_to_all | solution.py:72
  83.8 5.0 %stack.3 = bf16[4,2,1792,256]{2,3,1,0:T(8,128)(2,1)} broadcast(bf16[2,1792,256]{1,2,0:T(8,128)(2,1)} %copy.63), dimensions={1,2,3} | broadcast | bytes 9175040 | tf_op jit(solution)/shard_map/stack | solution.py:79
  88.8 5.5 %all-to-all-start.1 = ((bf16[4,2,1792,256]{2,3,1,0:T(8,128)(2,1)}), bf16[4,2,1792,256]{2,3,1,0:T(8,128)(2,1)}, u32[]{:S(2)}, u32[]{:S(2)}) async-start(bf16[4,2,1792,256]{2,3,1,0:T(8,128)(2,1)} %stack.3), calls=%async_computation.1 | async-start | bytes 14680064 | tf_op jit(solution)/shard_map/all_to_all | solution.py:79
  94.3 0.0 all-gather.3.cloned.1.call-start
  94.3 0.7 all-gather.3.cloned.1.call-update
  95.0 0.4 reshape.114
  95.4 110.0 %all-to-all-done.1 = bf16[4,2,1792,256]{2,3,1,0:T(8,128)(2,1)} async-done(((bf16[4,2,1792,256]{2,3,1,0:T(8,128)(2,1)}), bf16[4,2,1792,256]{2,3,1,0:T(8,128)(2,1)}, u32[]{:S(2)}, u32[]{:S(2)}) %all-to-all-start.1) | async-done | bytes 7340064 | tf_op jit(solution)/shard_map/all_to_all | solution.py:79
  205.4 5.3 %fusion.8 = f32[4,384,2,256]{3,1,0,2:T(8,128)S(1)} fusion(bf16[4,2,1792,256]{2,3,1,0:T(8,128)(2,1)} %all-to-all-done.1, bf16[384,1792,1,1]{1,0,2,3:T(8,128)(2,1)S(1)} %reshape.114), kind=kOutput, calls=%fused_computation.8 | convolution fusion | flops 2818572288 | bytes 11862016 | tf_op jit(solution)/shard_map/rd,gdf->rgf/dot_general | solution.py:75
  210.7 0.2 copy.65
  210.9 57.9 %all_to_all.20 = f32[4,384,2,256]{3,1,2,0:T(8,128)S(1)} all-to-all(f32[4,384,2,256]{3,1,2,0:T(8,128)S(1)} %copy.65), channel_id=1, replica_groups=mesh['dp'=4,'expert'=32,'tensor_0'=2,'tensor_1'=2] {'tensor_0','tensor_1'}, dimensions={0} | all-to-all | bytes 6291456 | tf_op jit(solution)/shard_map/all_to_all | solution.py:23
  268.8 1.2 reduce_sum.52
  269.9 1.2 fusion.17
  271.2 23.5 %all_gather.9 = bf16[2,384,1,256]{3,1,2,0:T(8,128)(2,1)S(1)} all-gather(bf16[1,384,1,256]{3,1,2,0:T(8,128)(2,1)S(1)} %fusion.17), channel_id=1, replica_groups=mesh['dp'=4,'expert'=32,'tensor_0'=2,'tensor_1'=2] {'tensor_0'}, dimensions={0}, use_global_device_ids=true | all-gather | bytes 589824 | tf_op jit(solution)/shard_map/all_gather | solution.py:36
  294.7 2.4 all_gather.10
  297.1 0.1 copy.66
  297.1 0.4 copy.67
  297.5 0.0 all-gather.3.cloned.1.call-done
  297.5 3.7 fusion.5
  301.2 0.4 reshape.111
  301.5 64.4 %all_to_all.21 = bf16[32,12,1792]{2,1,0:T(8,128)(2,1)} all-to-all(bf16[32,12,1792]{2,1,0:T(8,128)(2,1)S(1)} %reshape.111), channel_id=1, replica_groups=mesh['dp'=4,'expert'=32,'tensor_0'=2,'tensor_1'=2] {'expert'}, dimensions={0} | all-to-all | bytes 2752512 | tf_op jit(solution)/shard_map/all_to_all | solution.py:94
  366.0 2.4 reshape.112
  368.3 1.2 convolution_convert_fusion.1
  (4 shorter events, 0.1 us)
Async XLA Ops:
  25.8 58.0 %all-to-all-start = ((bf16[32,12,1792]{2,1,0:T(8,128)(2,1)}), bf16[32,12,1792]{2,1,0:T(8,128)(2,1)S(1)}, u32[]{:S(2)}, u32[]{:S(2)}) async-start(bf16[32,12,1792]{2,1,0:T(8,128)(2,1)} %reshape.105), calls=%async_computation | async-start | bytes 3670016 | tf_op jit(solution)/shard_map/all_to_all | solution.py:72
  88.8 116.6 %all-to-all-start.1 = ((bf16[4,2,1792,256]{2,3,1,0:T(8,128)(2,1)}), bf16[4,2,1792,256]{2,3,1,0:T(8,128)(2,1)}, u32[]{:S(2)}, u32[]{:S(2)}) async-start(bf16[4,2,1792,256]{2,3,1,0:T(8,128)(2,1)} %stack.3), calls=%async_computation.1 | async-start | bytes 14680064 | tf_op jit(solution)/shard_map/all_to_all | solution.py:79
  94.3 203.2 %all-gather.3.cloned.1.call-start = ((), (), s32[]{:S(2)}) async-start(), calls=%async_computation.4 | async-start | bytes 4587520 | tf_op jit(solution)/shard_map/all_gather | solution.py:90
Sparse Core Ops, SparseCore 0:
  97.2 79.2 all-gather.2
